TPU v7x, 32 devices: a whole 2x2x4 slice. The times are simulated.
32 devices in a mesh: lon: 8 (over z, core), lat: 4 (over y, x).
Axes of the slice: x: 2, y: 2, z: 4, core: 2. Of those that a mesh axis runs over, the one named last changes fastest.
Arguments:
- tracers: float32 [32, 32, 16384], P(None, 'lat', 'lon'), may hold values from 0.1 to 10
- courant: float32 [2, 32, 256], P(None, 'lat', 'lon'), may hold values from -0.45 to 0.45
- switches: int32 [2, 32, 256], P(None, 'lat', 'lon'), may hold values 0 or 1
- day_flags: int32 [32, 256], P('lat', 'lon'), may hold values from 0 to 1, as said below
- diffusion_counts: int32 [32, 256], P('lat', 'lon'), may hold values from 1 to 8
- night_rates: float32 [32, 32], replicated, may hold values from -0.18 to 0.18
- photo_rates: float32 [32, 32], replicated, may hold values from -0.24 to 0.24
- level_light: float32 [64], replicated, may hold values from 0.1 to 1
- self_loss: float32 [32], replicated, may hold values from 0.001 to 0.05
- vertical_mixing: float32 [63], replicated, may hold values from 0.05 to 0.45
Outputs:
- tracers_out: float32 [32, 32, 16384], P(None, 'lat', 'lon')
Inputs may be any that keep to these rules, and one draw needn't show every extreme that they name: `day_flags`: in every latitude row exactly half of the 256 columns are day columns, forming one contiguous band around the longitude cycle.
All inputs are finite; a program needn't handle non-finite values. No bound on the sum of `switches` on one device may be relied on, other than what follows from the above.
Results may differ from a plain program's by a relative error of at most 0.0003.
Values sent between devices are 32-bit elements; how exact they have to be, the bound alone decides.
A program may use at most 64 MiB of HBM per device.

v0:
```python
import functools

import jax
import jax.numpy as jnp
from jax import lax
from jax.experimental import pallas as pl
from jax.experimental.pallas import tpu as pltpu
from jax.sharding import PartitionSpec as P

CHEM = 6
KMAX = 8
WIDE = 512
MESH = pl.DeviceIdType.MESH


def minmod(x, y):
    return jnp.maximum(jnp.minimum(x, y), 0.0) + jnp.minimum(jnp.maximum(x, y), 0.0)


def face_flux(c, coef, aa, a, b, bb):
    pos = c >= 0.0
    x = jnp.where(pos, a - aa, bb - b)
    return c * (jnp.where(pos, a, b) + coef * minmod(x, b - a))


def kernel(
    unit,
    x_ref,
    lonc_ref,
    lonk_ref,
    latc_ref,
    latk_ref,
    sun_ref,
    cnt_ref,
    mix_ref,
    w_ref,
    loss_ref,
    out_ref,
    mid_ref,
    state_ref,
    again_ref,
    west_ref,
    east_ref,
    south_ref,
    north_ref,
    lon_send,
    lon_recv,
    lat_send,
    lat_recv,
):
    rows, species, lanes = x_ref.shape
    tiles = lanes // unit
    edge = 2
    nlon, nlat = lax.axis_size("lon"), lax.axis_size("lat")
    lon, lat = lax.axis_index("lon"), lax.axis_index("lat")
    east, west = lax.rem(lon + 1, nlon), lax.rem(lon + nlon - 1, nlon)
    has_south, has_north = lat > 0, lat < nlat - 1

    barrier = pltpu.get_barrier_semaphore()
    for side in (east, west):
        pl.semaphore_signal(barrier, inc=1, device_id={"lon": side}, device_id_type=MESH)

    @pl.when(has_south)
    def _():
        pl.semaphore_signal(barrier, inc=1, device_id={"lat": lat - 1}, device_id_type=MESH)

    @pl.when(has_north)
    def _():
        pl.semaphore_signal(barrier, inc=1, device_id={"lat": lat + 1}, device_id_type=MESH)

    @pl.when(jnp.logical_not(has_south))
    def _():
        south_ref[...] = jnp.zeros_like(south_ref)
        pl.semaphore_wait(barrier, 3)

    @pl.when(jnp.logical_not(has_north))
    def _():
        north_ref[...] = jnp.zeros_like(north_ref)
        pl.semaphore_wait(barrier, 3)

    @pl.when(jnp.logical_and(has_south, has_north))
    def _():
        pl.semaphore_wait(barrier, 4)

    groups = ((0, edge), (rows - edge, edge), (edge, rows - 2 * edge))

    def lon_copies(source, turn, group):
        first, number = groups[group]
        held = pl.ds(first, number)
        pairs = (
            (source.at[held, :, pl.ds(lanes - unit, unit)], west_ref.at[turn, held], east),
            (source.at[held, :, pl.ds(0, unit)], east_ref.at[turn, held], west),
        )
        return [
            pltpu.make_async_remote_copy(
                src_ref=src,
                dst_ref=dst,
                send_sem=lon_send.at[turn, group, way],
                recv_sem=lon_recv.at[turn, group, way],
                device_id={"lon": to},
                device_id_type=MESH,
            )
            for way, (src, dst, to) in enumerate(pairs)
        ]

    def lat_copies(source, turn):
        up = pltpu.make_async_remote_copy(
            src_ref=source.at[pl.ds(rows - edge, edge)],
            dst_ref=south_ref.at[turn],
            send_sem=lat_send.at[turn, 0],
            recv_sem=lat_recv.at[turn, 0],
            device_id={"lat": lat + 1},
            device_id_type=MESH,
        )
        down = pltpu.make_async_remote_copy(
            src_ref=source.at[pl.ds(0, edge)],
            dst_ref=north_ref.at[turn],
            send_sem=lat_send.at[turn, 1],
            recv_sem=lat_recv.at[turn, 1],
            device_id={"lat": lat - 1},
            device_id_type=MESH,
        )
        return up, down

    def lat_start(source, turn):
        up, down = lat_copies(source, turn)

        @pl.when(has_north)
        def _():
            up.start()

        @pl.when(has_south)
        def _():
            down.start()

    def lat_wait(source, turn):
        up, down = lat_copies(source, turn)

        @pl.when(has_north)
        def _():
            up.wait_send()
            down.wait_recv()

        @pl.when(has_south)
        def _():
            down.wait_send()
            up.wait_recv()

    def edge_row(i):
        return i + (i // edge) * (rows - 2 * edge)

    low = lax.broadcasted_iota(jnp.int32, (species, unit), 1) < unit // 2

    def lon_sweep(source, target, turn, number, row_of):
        def one(i, carry):
            row = row_of(i)

            def tile(j):
                if j < 0:
                    return west_ref[turn, row]
                if j == tiles:
                    return east_ref[turn, row]
                return source[row, :, j * unit : (j + 1) * unit]

            def swap(v):
                return pltpu.roll(v, unit // 2, 1)

            before, here = tile(-1), tile(0)
            swapped = swap(here)
            behind = jnp.where(low, swap(before), swapped)
            flux, turned, cell = None, None, None
            for j in range(tiles + 1):
                if j < tiles:
                    after = tile(j + 1)
                    after_swapped = swap(after)
                    ahead = jnp.where(low, swapped, after_swapped)
                else:
                    after, after_swapped, ahead = here, swapped, swapped
                at = slice(j * unit, (j + 1) * unit)
                c = lonc_ref[row, :, at]
                k = lonk_ref[row, :, at]
                now = face_flux(c, k, before, behind, here, ahead)
                now_turned = swap(now)
                if j > 0:
                    upper = jnp.where(low, turned, now_turned)
                    target[row, :, (j - 1) * unit : j * unit] = cell - (upper - flux)
                flux, turned, cell = now, now_turned, here
                before, here, behind, swapped = here, after, ahead, after_swapped
            return carry

        lax.fori_loop(0, number, one, 0)

    def lat_sweep(source, target, turn, spans):
        def one(j, carry):
            at = pl.ds(pl.multiple_of(j * unit, unit), unit)

            def cell(row):
                if row < 0:
                    return south_ref[turn, row + edge, :, at]
                if row >= rows:
                    return north_ref[turn, row - rows, :, at]
                return source[row, :, at]

            for first, last in spans:
                aa, a, b = cell(first - 2), cell(first - 1), cell(first)
                flux = None
                for row in range(first, last + 1):
                    bb = cell(row + 1)
                    c = latc_ref[row, :, at]
                    k = latk_ref[row, :, at]
                    now = face_flux(c, k, aa, a, b, bb)
                    if flux is not None:
                        target[row - 1, :, at] = a - (now - flux)
                    flux = now
                    aa, a, b = a, b, bb
            return carry

        lax.fori_loop(0, tiles, one, 0)

    wide = min(WIDE, lanes)
    pieces = lanes // wide

    def chemistry(number, row_of):
        def one(i, carry):
            row = row_of(i // pieces)
            start = pl.multiple_of((i % pieces) * wide, wide)
            at = pl.ds(start, wide)
            q = state_ref[row, :, at]
            sun = sun_ref[row, :, at]
            loss = loss_ref[...]
            for _ in range(CHEM):
                high = q.astype(jnp.bfloat16)
                rest = (q - high.astype(jnp.float32)).astype(jnp.bfloat16)
                both = jnp.dot(
                    w_ref[...],
                    jnp.concatenate([high, rest, high], 0),
                    preferred_element_type=jnp.float32,
                )
                q = (q + both[:species] + sun * both[species:]) / (1.0 + loss * q * q)
            for t in range(wide // unit):
                v = q[:, t * unit : (t + 1) * unit]
                here = pl.ds(start + t * unit, unit)
                count = cnt_ref[row, :, here]
                for step in range(KMAX):
                    m = jnp.where(step < count, mix_ref[...], 0.0)
                    flow = m * (pltpu.roll(v, unit - 1, 1) - v)
                    v = v + flow - pltpu.roll(flow, 1, 1)
                state_ref[row, :, here] = v
            return carry

        lax.fori_loop(0, number * pieces, one, 0)

    inner = rows - 2 * edge
    edge_spans = ((0, edge), (rows - edge, rows))
    inner_spans = ((edge, rows - edge),)

    def inner_row(i):
        return i + edge

    first = [lon_copies(x_ref, 0, group) for group in range(3)]
    for pair in first:
        for copy in pair:
            copy.start()
    for pair in first[:2]:
        for copy in pair:
            copy.wait()
    lon_sweep(x_ref, mid_ref, 0, 2 * edge, edge_row)
    lat_start(mid_ref, 0)
    for copy in first[2]:
        copy.wait()
    lon_sweep(x_ref, mid_ref, 0, inner, inner_row)
    lat_sweep(mid_ref, state_ref, 0, inner_spans)
    chemistry(inner, inner_row)
    second = [lon_copies(state_ref, 1, group) for group in range(3)]
    for copy in second[2]:
        copy.start()
    lat_wait(mid_ref, 0)
    lat_sweep(mid_ref, state_ref, 0, edge_spans)
    chemistry(2 * edge, edge_row)
    for pair in second[:2]:
        for copy in pair:
            copy.start()
    for pair in second[:2]:
        for copy in pair:
            copy.wait()
    lon_sweep(state_ref, again_ref, 1, 2 * edge, edge_row)
    lat_start(again_ref, 1)
    for copy in second[2]:
        copy.wait()
    lon_sweep(state_ref, again_ref, 1, inner, inner_row)
    lat_sweep(again_ref, out_ref, 1, inner_spans)
    lat_wait(again_ref, 1)
    lat_sweep(again_ref, out_ref, 1, edge_spans)


def shifted(value, axis, steps):
    count = lax.axis_size(axis)
    return lax.ppermute(value, axis, [(i, (i + steps) % count) for i in range(count)])


def from_ahead(value, axis):
    count = lax.axis_size(axis)
    return lax.ppermute(value, axis, [(i + 1, i) for i in range(count - 1)])


def slopes(c, m):
    return jnp.where(c >= 0.0, 0.5 * (1.0 - c), -0.5 * (1.0 + c)) * m


def shards(
    tracers,
    courant,
    switches,
    day_flags,
    diffusion_counts,
    night_rates,
    photo_rates,
    level_light,
    self_loss,
    vertical_mixing,
):
    species, rows, lanes = tracers.shape
    levels = level_light.shape[0]
    columns = lanes // levels
    unit = 2 * levels
    f32 = jnp.float32
    nlat = lax.axis_size("lat")
    faces = jnp.concatenate([courant, switches.astype(f32)], 0)
    east_faces = shifted(faces[0::2, :, :1], "lon", -1)
    north_faces = from_ahead(faces[1::2, :1], "lat")
    lon_faces = jnp.concatenate([faces[0::2], east_faces, east_faces], 2)
    lat_faces = jnp.concatenate([faces[1::2], north_faces], 1)
    global_face = lax.axis_index("lat") * rows + jnp.arange(rows + 1, dtype=jnp.int32)
    valid = ((global_face >= 1) & (global_face < rows * nlat)).astype(f32)[:, None]
    lat_c = lat_faces[0] * valid
    spread = functools.partial(jnp.repeat, repeats=levels, axis=-1)
    lon_c = spread(lon_faces[0])
    lon_k = spread(slopes(lon_faces[0], lon_faces[1]))
    lat_k = spread(slopes(lat_c, lat_faces[1]))
    lat_c = spread(lat_c)
    sun = spread(day_flags.astype(f32)) * jnp.tile(level_light, columns)
    counts = spread(diffusion_counts)
    mixing = jnp.concatenate([vertical_mixing, jnp.zeros((1,), f32)])
    mixing = jnp.tile(mixing, 2)[None]
    rates = jnp.concatenate([night_rates, photo_rates], 0)
    top = lax.reduce_precision(rates, 8, 7)
    rest = (rates - top).astype(jnp.bfloat16)
    top = top.astype(jnp.bfloat16)
    weights = jnp.concatenate([top, top, rest], 1)
    block = (rows, species, lanes)
    out = pl.pallas_call(
        functools.partial(kernel, unit),
        out_shape=jax.ShapeDtypeStruct(block, f32),
        in_specs=[pl.BlockSpec(memory_space=pltpu.VMEM)] * 10,
        out_specs=pl.BlockSpec(memory_space=pltpu.VMEM),
        scratch_shapes=[
            pltpu.VMEM(block, f32),
            pltpu.VMEM(block, f32),
            pltpu.VMEM(block, f32),
            pltpu.VMEM((2, rows, species, unit), f32),
            pltpu.VMEM((2, rows, species, unit), f32),
            pltpu.VMEM((2, 2, species, lanes), f32),
            pltpu.VMEM((2, 2, species, lanes), f32),
            pltpu.SemaphoreType.DMA((2, 3, 2)),
            pltpu.SemaphoreType.DMA((2, 3, 2)),
            pltpu.SemaphoreType.DMA((2, 2)),
            pltpu.SemaphoreType.DMA((2, 2)),
        ],
        compiler_params=pltpu.CompilerParams(
            collective_id=0, has_side_effects=True, vmem_limit_bytes=48 * 1024 * 1024
        ),
    )(
        jnp.transpose(tracers, (1, 0, 2)),
        lon_c[:, None],
        lon_k[:, None],
        lat_c[:, None],
        lat_k[:, None],
        sun[:, None],
        counts[:, None],
        mixing,
        weights,
        self_loss[:, None],
    )
    return jnp.transpose(out, (1, 0, 2))


def solution(mesh):
    grid = P(None, "lat", "lon")
    plane = P("lat", "lon")
    in_specs = (grid, grid, grid, plane, plane, P(), P(), P(), P(), P())
    return jax.shard_map(shards, mesh=mesh, in_specs=in_specs, out_specs=grid, check_vma=False)
```

profile of v0, /device:TPU:0, one launch (start us, length us, event | category | flops | bytes accessed | tf_op | source)
XLA Modules:
  0.0 124.9 jit_solution(12801493960044950509)
XLA Ops:
  0.0 0.7 convert_element_type.19
  0.7 0.7 pad_maximum_fusion
  1.4 1.3 %collective-permute-start.1 = (f32[2,1,32]{2,1,0:T(1,128)S(1)}, f32[2,1,32]{2,1,0:T(1,128)S(1)}, u32[]{:S(2)}, u32[]{:S(2)}) collective-permute-start(f32[2,1,32]{2,1,0:T(1,128)S(1)} %slice.30), channel_id=1, source_target_pairs={{1,0},{2,1},{3,2},{5,4},{6,5},{7,6},{9,8},{10,9},{11,10},{13,12},{... | collective-permute-start | bytes 776 | tf_op jit(solution)/shard_map/ppermute | solution.py:303
  2.7 4.6 %collective-permute-start = (f32[2,8,1]{2,1,0:T(8,128)S(1)}, f32[2,8,1]{2,1,0:T(8,128)S(1)}, u32[]{:S(2)}, u32[]{:S(2)}) collective-permute-start(f32[2,8,1]{2,1,0:T(8,128)S(1)} %slice.26), channel_id=1, source_target_pairs={{0,28},{4,0},{8,4},{12,8},{16,12},{20,16},{24,20},{28,24},{1,29},{... | collective-permute-start | bytes 200 | tf_op jit(solution)/shard_map/ppermute | solution.py:298
  7.3 0.7 pad_maximum_fusion.4
  8.0 0.1 broadcast_in_dim_tile.4.mix_ref
  8.1 0.7 convert_element_type.21
  8.8 0.7 tile.4
  9.4 0.1 mul.71
  9.5 0.7 copy.17.loss_ref
  10.3 0.7 constant_dynamic-update-slice_fusion.1
  11.0 0.7 constant_dynamic-update-slice_fusion
  11.7 0.1 broadcast_in_dim.27
  11.8 0.1 reshape.52
  11.9 0.8 broadcast_in_dim.28
  12.7 0.1 broadcast_in_dim_reshape.19.cnt_ref
  12.9 0.1 pad_maximum_fusion.1.w_ref
  12.9 0.1 broadcast_multiply_fusion.sun_ref
  13.0 2.8 %copy.20 = f32[32,8,2048]{2,0,1:T(8,128)S(1)} copy(f32[32,8,2048]{2,1,0:T(8,128)} %param.10) | data formatting | bytes 4194304 | tf_op args[0]
  15.8 0.0 collective-permute-done
  15.8 0.1 pad_maximum_fusion.3
  15.9 0.1 broadcast_in_dim.23
  16.0 0.1 broadcast_in_dim_reshape.20.lonc_ref
  16.2 0.1 broadcast_in_dim.24
  16.3 0.1 broadcast_in_dim_reshape.21.lonk_ref
  16.4 0.0 collective-permute-done.1
  16.4 0.1 fusion.5
  16.5 0.1 broadcast_in_dim.26
  16.6 0.1 broadcast_in_dim_reshape.18.latk_ref
  16.8 0.1 broadcast_in_dim.25
  16.9 0.1 broadcast_in_dim_reshape.17.latc_ref
  17.0 105.3 %shard_map.100 = f32[8,32,2048]{2,1,0:T(8,128)S(1)} custom-call(f32[8,32,2048]{2,1,0:T(8,128)S(1)} %bitcast.22, f32[8,1,2176]{2,1,0:T(1,128)S(1)} %broadcast_in_dim_reshape.20.lonc_ref, f32[8,1,2176]{2,1,0:T(1,128)S(1)} %broadcast_in_dim_reshape.21.lonk_ref, f32[9,1,2048]{2,1,0:T(1,128)S(1)} %broadcast_in_dim_reshape.17.latc_ref, ...), custom_call_target="tpu_custom_call" | custom-call | tf_op jit(solution)/shard_map/pallas_call | solution.py:351
  122.3 2.5 %copy.18 = f32[32,8,2048]{2,1,0:T(8,128)} copy(f32[32,8,2048]{2,0,1:T(8,128)S(1)} %bitcast.23) | data formatting | bytes 4194304 | tf_op jit(solution)/shard_map/transpose | solution.py:384
  (8 shorter events, 0.0 us)
Async XLA Ops:
  1.4 15.0 %collective-permute-start.1 = (f32[2,1,32]{2,1,0:T(1,128)S(1)}, f32[2,1,32]{2,1,0:T(1,128)S(1)}, u32[]{:S(2)}, u32[]{:S(2)}) collective-permute-start(f32[2,1,32]{2,1,0:T(1,128)S(1)} %slice.30), channel_id=1, source_target_pairs={{1,0},{2,1},{3,2},{5,4},{6,5},{7,6},{9,8},{10,9},{11,10},{13,12},{... | collective-permute-start | bytes 776 | tf_op jit(solution)/shard_map/ppermute | solution.py:303
  2.7 13.1 %collective-permute-start = (f32[2,8,1]{2,1,0:T(8,128)S(1)}, f32[2,8,1]{2,1,0:T(8,128)S(1)}, u32[]{:S(2)}, u32[]{:S(2)}) collective-permute-start(f32[2,8,1]{2,1,0:T(8,128)S(1)} %slice.26), channel_id=1, source_target_pairs={{0,28},{4,0},{8,4},{12,8},{16,12},{20,16},{24,20},{28,24},{1,29},{... | collective-permute-start | bytes 200 | tf_op jit(solution)/shard_map/ppermute | solution.py:298
where the time goes:
time: 125 us
  Pallas kernels  105 us (84%)
  local copies, waits for them, and re-layouts  10.4 us (8%)
  starting transfers between devices  5.85 us (5%)
  other arithmetic  3.13 us (3%)
    pallas_call x1, Pallas kernels, shards(): pl.pallas_call(functools.partial(kernel, unit), out_shape=jax.ShapeDtypeS...  105 us
    ppermute x1, starting transfers between devices, shifted(): lax.ppermute(value, axis, [(i, (i + steps) % count) for i in range(count)])  4.57 us
    unnamed x2, local copies, waits for them, and re-layouts  3.53 us
    transpose x1, local copies, waits for them, and re-layouts, shards(): return jnp.transpose(out, (1, 0, 2))  2.54 us
  transfers between devices with their start and end apart: 2, of which 0 were waited for; matrix products, arithmetic and copies ran while one was open for 7% of the time, Pallas kernels for 0%

commit v1 on v0

--- a/solution.py
+++ b/solution.py
@@ -9,7 +9,7 @@
 
 CHEM = 6
 KMAX = 8
-WIDE = 512
+WIDE = 2048
 MESH = pl.DeviceIdType.MESH
 
 
@@ -21,6 +21,31 @@
     pos = c >= 0.0
     x = jnp.where(pos, a - aa, bb - b)
     return c * (jnp.where(pos, a, b) + coef * minmod(x, b - a))
+
+
+def build_powers(unit, mix_ref, power_ref):
+    source = lax.broadcasted_iota(jnp.int32, (unit, unit), 0)
+    target = lax.broadcasted_iota(jnp.int32, (unit, unit), 1)
+    up = jnp.broadcast_to(mix_ref[...], (unit, unit))
+    down = pltpu.roll(up, 1, 1)
+    one = jnp.where(source == target, 1.0 - up - down, 0.0)
+    one = jnp.where(source == target + 1, up, one)
+    one = jnp.where(source == target - 1, down, one)
+    powers = {1: one}
+    for n in range(2, KMAX + 1):
+        half = n // 2
+        powers[n] = jnp.dot(
+            powers[half],
+            powers[n - half],
+            precision=lax.Precision.HIGHEST,
+            preferred_element_type=jnp.float32,
+        )
+    for n, power in powers.items():
+        at = slice((n - 1) * unit, n * unit)
+        top = power.astype(jnp.bfloat16)
+        power_ref[:unit, at] = top
+        power_ref[unit : 2 * unit, at] = top
+        power_ref[2 * unit :, at] = (power - top.astype(jnp.float32)).astype(jnp.bfloat16)
 
 
 def kernel(
@@ -43,6 +68,7 @@
     east_ref,
     south_ref,
     north_ref,
+    power_ref,
     lon_send,
     lon_recv,
     lat_send,
@@ -237,15 +263,27 @@
                     preferred_element_type=jnp.float32,
                 )
                 q = (q + both[:species] + sun * both[species:]) / (1.0 + loss * q * q)
-            for t in range(wide // unit):
-                v = q[:, t * unit : (t + 1) * unit]
-                here = pl.ds(start + t * unit, unit)
-                count = cnt_ref[row, :, here]
-                for step in range(KMAX):
-                    m = jnp.where(step < count, mix_ref[...], 0.0)
-                    flow = m * (pltpu.roll(v, unit - 1, 1) - v)
-                    v = v + flow - pltpu.roll(flow, 1, 1)
-                state_ref[row, :, here] = v
+            spots = range(wide // unit)
+            q = jnp.concatenate([q[:, t * unit : (t + 1) * unit] for t in spots], 0)
+            high = q.astype(jnp.bfloat16)
+            rest = (q - high.astype(jnp.float32)).astype(jnp.bfloat16)
+            terms = jnp.concatenate([high, rest, high], 1)
+            mixed = [None for t in spots]
+            for n in range(0, KMAX, 2):
+                both = jnp.dot(
+                    terms,
+                    power_ref[:, n * unit : (n + 2) * unit],
+                    preferred_element_type=jnp.float32,
+                )
+                for t in spots:
+                    held = slice(t * species, (t + 1) * species)
+                    count = cnt_ref[row, :, pl.ds(start + t * unit, unit)]
+                    v = both[held, :unit]
+                    if n > 0:
+                        v = jnp.where(count > n, v, mixed[t])
+                    mixed[t] = jnp.where(count > n + 1, both[held, unit:], v)
+            for t in spots:
+                state_ref[row, :, pl.ds(start + t * unit, unit)] = mixed[t]
             return carry
 
         lax.fori_loop(0, number * pieces, one, 0)
@@ -261,6 +299,7 @@
     for pair in first:
         for copy in pair:
             copy.start()
+    build_powers(unit, mix_ref, power_ref)
     for pair in first[:2]:
         for copy in pair:
             copy.wait()
@@ -361,6 +400,7 @@
             pltpu.VMEM((2, rows, species, unit), f32),
             pltpu.VMEM((2, 2, species, lanes), f32),
             pltpu.VMEM((2, 2, species, lanes), f32),
+            pltpu.VMEM((3 * unit, KMAX * unit), jnp.bfloat16),
             pltpu.SemaphoreType.DMA((2, 3, 2)),
             pltpu.SemaphoreType.DMA((2, 3, 2)),
             pltpu.SemaphoreType.DMA((2, 2)),

time: 125 us -> 88.1 us (0.70)
  Pallas kernels: 105 us -> 68 us
    pallas_call x1, Pallas kernels: 105 us -> 68 us  [shards(): pl.pallas_call(functools.partial(kernel, unit), out_shape=jax.ShapeDtypeS...]
  transfers between devices with their start and end apart: 2 -> 2, of which waited for: 0 -> 0; matrix products, arithmetic and copies ran while one was open for 7% -> 10% of each run, Pallas kernels for 0% -> 0%
where the time goes in v1:
time: 88.1 us; the launch traced here: 87.6 us
  Pallas kernels  68 us (77%)
  local copies, waits for them, and re-layouts  10.4 us (12%)
  starting transfers between devices  5.85 us (7%)
  other arithmetic  3.13 us (4%)
    pallas_call x1, Pallas kernels, shards(): pl.pallas_call(functools.partial(kernel, unit), out_shape=jax.ShapeDtypeS...  68 us
    ppermute x1, starting transfers between devices, shifted(): lax.ppermute(value, axis, [(i, (i + steps) % count) for i in range(count)])  4.57 us
    unnamed x2, local copies, waits for them, and re-layouts  3.53 us
    transpose x1, local copies, waits for them, and re-layouts, shards(): return jnp.transpose(out, (1, 0, 2))  2.54 us
  transfers between devices with their start and end apart: 2, of which 0 were waited for; matrix products, arithmetic and copies ran while one was open for 10% of the time, Pallas kernels for 0%

profile of v1, /device:TPU:0, one launch (start us, length us, event | category | flops | bytes accessed | tf_op | source)
XLA Modules:
  0.0 87.6 jit_solution(16087422697734826541)
XLA Ops:
  0.0 0.7 convert_element_type.19
  0.7 0.7 pad_maximum_fusion
  1.4 1.3 %collective-permute-start.1 = (f32[2,1,32]{2,1,0:T(1,128)S(1)}, f32[2,1,32]{2,1,0:T(1,128)S(1)}, u32[]{:S(2)}, u32[]{:S(2)}) collective-permute-start(f32[2,1,32]{2,1,0:T(1,128)S(1)} %slice.30), channel_id=1, source_target_pairs={{1,0},{2,1},{3,2},{5,4},{6,5},{7,6},{9,8},{10,9},{11,10},{13,12},{... | collective-permute-start | bytes 776 | tf_op jit(solution)/shard_map/ppermute | solution.py:342
  2.7 4.6 %collective-permute-start = (f32[2,8,1]{2,1,0:T(8,128)S(1)}, f32[2,8,1]{2,1,0:T(8,128)S(1)}, u32[]{:S(2)}, u32[]{:S(2)}) collective-permute-start(f32[2,8,1]{2,1,0:T(8,128)S(1)} %slice.26), channel_id=1, source_target_pairs={{0,28},{4,0},{8,4},{12,8},{16,12},{20,16},{24,20},{28,24},{1,29},{... | collective-permute-start | bytes 200 | tf_op jit(solution)/shard_map/ppermute | solution.py:337
  7.3 0.7 pad_maximum_fusion.4
  8.0 0.1 broadcast_in_dim_tile.4.mix_ref
  8.1 0.7 convert_element_type.21
  8.8 0.7 tile.4
  9.4 0.1 mul.71
  9.5 0.7 copy.17.loss_ref
  10.3 0.7 constant_dynamic-update-slice_fusion.1
  11.0 0.7 constant_dynamic-update-slice_fusion
  11.7 0.1 broadcast_in_dim.27
  11.8 0.1 reshape.52
  11.9 0.8 broadcast_in_dim.28
  12.7 0.1 broadcast_in_dim_reshape.19.cnt_ref
  12.9 0.1 pad_maximum_fusion.1.w_ref
  12.9 0.1 broadcast_multiply_fusion.sun_ref
  13.0 2.8 %copy.20 = f32[32,8,2048]{2,0,1:T(8,128)S(1)} copy(f32[32,8,2048]{2,1,0:T(8,128)} %param.10) | data formatting | bytes 4194304 | tf_op args[0]
  15.8 0.0 collective-permute-done
  15.8 0.1 pad_maximum_fusion.3
  15.9 0.1 broadcast_in_dim.23
  16.0 0.1 broadcast_in_dim_reshape.20.lonc_ref
  16.2 0.1 broadcast_in_dim.24
  16.3 0.1 broadcast_in_dim_reshape.21.lonk_ref
  16.4 0.0 collective-permute-done.1
  16.4 0.1 fusion.5
  16.5 0.1 broadcast_in_dim.26
  16.6 0.1 broadcast_in_dim_reshape.18.latk_ref
  16.8 0.1 broadcast_in_dim.25
  16.9 0.1 broadcast_in_dim_reshape.17.latc_ref
  17.0 68.0 %shard_map.100 = f32[8,32,2048]{2,1,0:T(8,128)S(1)} custom-call(f32[8,32,2048]{2,1,0:T(8,128)S(1)} %bitcast.22, f32[8,1,2176]{2,1,0:T(1,128)S(1)} %broadcast_in_dim_reshape.20.lonc_ref, f32[8,1,2176]{2,1,0:T(1,128)S(1)} %broadcast_in_dim_reshape.21.lonk_ref, f32[9,1,2048]{2,1,0:T(1,128)S(1)} %broadcast_in_dim_reshape.17.latc_ref, ...), custom_call_target="tpu_custom_call" | custom-call | tf_op jit(solution)/shard_map/pallas_call | solution.py:390
  85.0 2.5 %copy.18 = f32[32,8,2048]{2,1,0:T(8,128)} copy(f32[32,8,2048]{2,0,1:T(8,128)S(1)} %bitcast.23) | data formatting | bytes 4194304 | tf_op jit(solution)/shard_map/transpose | solution.py:424
  (8 shorter events, 0.0 us)
Async XLA Ops:
  1.4 15.0 %collective-permute-start.1 = (f32[2,1,32]{2,1,0:T(1,128)S(1)}, f32[2,1,32]{2,1,0:T(1,128)S(1)}, u32[]{:S(2)}, u32[]{:S(2)}) collective-permute-start(f32[2,1,32]{2,1,0:T(1,128)S(1)} %slice.30), channel_id=1, source_target_pairs={{1,0},{2,1},{3,2},{5,4},{6,5},{7,6},{9,8},{10,9},{11,10},{13,12},{... | collective-permute-start | bytes 776 | tf_op jit(solution)/shard_map/ppermute | solution.py:342
  2.7 13.1 %collective-permute-start = (f32[2,8,1]{2,1,0:T(8,128)S(1)}, f32[2,8,1]{2,1,0:T(8,128)S(1)}, u32[]{:S(2)}, u32[]{:S(2)}) collective-permute-start(f32[2,8,1]{2,1,0:T(8,128)S(1)} %slice.26), channel_id=1, source_target_pairs={{0,28},{4,0},{8,4},{12,8},{16,12},{20,16},{24,20},{28,24},{1,29},{... | collective-permute-start | bytes 200 | tf_op jit(solution)/shard_map/ppermute | solution.py:337

commit v2 on v1

--- a/solution.py
+++ b/solution.py
@@ -51,6 +51,16 @@
 def kernel(
     unit,
     x_ref,
+    courant_ref,
+    switch_ref,
+    day_ref,
+    raw_cnt_ref,
+    night_ref,
+    photo_ref,
+    light_ref,
+    raw_loss_ref,
+    vertical_ref,
+    out_ref,
     lonc_ref,
     lonk_ref,
     latc_ref,
@@ -60,7 +70,8 @@
     mix_ref,
     w_ref,
     loss_ref,
-    out_ref,
+    face_c_ref,
+    face_s_ref,
     mid_ref,
     state_ref,
     again_ref,
@@ -73,6 +84,8 @@
     lon_recv,
     lat_send,
     lat_recv,
+    face_send,
+    face_recv,
 ):
     rows, species, lanes = x_ref.shape
     tiles = lanes // unit
@@ -102,6 +115,8 @@
     @pl.when(jnp.logical_not(has_north))
     def _():
         north_ref[...] = jnp.zeros_like(north_ref)
+        face_c_ref[1] = jnp.zeros(face_c_ref.shape[1:], face_c_ref.dtype)
+        face_s_ref[1] = jnp.zeros(face_s_ref.shape[1:], face_s_ref.dtype)
         pl.semaphore_wait(barrier, 3)
 
     @pl.when(jnp.logical_and(has_south, has_north))
@@ -128,6 +143,79 @@
             )
             for way, (src, dst, to) in enumerate(pairs)
         ]
+
+    def face_copies(side, to):
+        pairs = ((courant_ref, face_c_ref), (switch_ref, face_s_ref))
+        return [
+            pltpu.make_async_remote_copy(
+                src_ref=src,
+                dst_ref=dst.at[side],
+                send_sem=face_send.at[side, n],
+                recv_sem=face_recv.at[side, n],
+                device_id=to,
+                device_id_type=MESH,
+            )
+            for n, (src, dst) in enumerate(pairs)
+        ]
+
+    lon_faces = face_copies(0, {"lon": west})
+    lat_faces = face_copies(1, {"lat": lat - 1})
+
+    def spread(plane, target, scale=None):
+        left = lax.broadcasted_iota(jnp.int32, (plane.shape[0], unit), 1) < unit // 2
+        for j in range(tiles):
+            a = jnp.broadcast_to(plane[:, 2 * j : 2 * j + 1], left.shape)
+            b = jnp.broadcast_to(plane[:, 2 * j + 1 : 2 * j + 2], left.shape)
+            v = jnp.where(left, a, b)
+            if scale is not None:
+                v = v * scale
+            for r in range(plane.shape[0]):
+                target(r, slice(j * unit, (j + 1) * unit), v[r : r + 1])
+
+    def into(ref, offset=0):
+        def put(r, at, v):
+            ref[r + offset, :, at] = v
+
+        return put
+
+    def prepare():
+        c = courant_ref[...]
+        m = switch_ref[...].astype(jnp.float32)
+        spread(c[0], into(lonc_ref))
+        spread(slopes(c[0], m[0]), into(lonk_ref))
+        row = lax.broadcasted_iota(jnp.int32, c[1].shape, 0)
+        lat_c = jnp.where(jnp.logical_and(row == 0, lat == 0), 0.0, c[1])
+        spread(lat_c, into(latc_ref))
+        spread(slopes(lat_c, m[1]), into(latk_ref))
+        mix = vertical_ref[...]
+        gap = jnp.zeros((1, 1), jnp.float32)
+        mix_ref[...] = jnp.concatenate([mix, gap, mix, gap], 1)
+        light = jnp.concatenate([light_ref[...], light_ref[...]], 1)
+        spread(day_ref[...].astype(jnp.float32), into(sun_ref), light)
+        spread(raw_cnt_ref[...], into(cnt_ref))
+
+    def prepare_outer():
+        c = face_c_ref[0, 0][:, :1]
+        k = slopes(c, face_s_ref[0, 0][:, :1].astype(jnp.float32))
+        c = jnp.broadcast_to(c, (rows, unit))
+        k = jnp.broadcast_to(k, (rows, unit))
+        for r in range(rows):
+            lonc_ref[r, :, lanes:] = c[r : r + 1]
+            lonk_ref[r, :, lanes:] = k[r : r + 1]
+
+    def prepare_north():
+        c = face_c_ref[1, 1][:1]
+        spread(c, into(latc_ref, rows))
+        spread(slopes(c, face_s_ref[1, 1][:1].astype(jnp.float32)), into(latk_ref, rows))
+
+    def prepare_rates():
+        rates = jnp.concatenate([night_ref[...], photo_ref[...]], 0)
+        top = rates.astype(jnp.bfloat16).astype(jnp.float32)
+        w_ref[...] = jnp.concatenate([top, top, rates - top], 1).astype(jnp.bfloat16)
+        shape = (species, species)
+        same = lax.broadcasted_iota(jnp.int32, shape, 0) == lax.broadcasted_iota(jnp.int32, shape, 1)
+        spread_loss = jnp.broadcast_to(raw_loss_ref[...], shape)
+        loss_ref[...] = jnp.sum(jnp.where(same, spread_loss, 0.0), axis=1, keepdims=True)
 
     def lat_copies(source, turn):
         up = pltpu.make_async_remote_copy(
@@ -295,16 +383,41 @@
     def inner_row(i):
         return i + edge
 
+    for copy in lon_faces:
+        copy.start()
+
+    @pl.when(has_south)
+    def _():
+        for copy in lat_faces:
+            copy.start()
+
     first = [lon_copies(x_ref, 0, group) for group in range(3)]
     for pair in first:
         for copy in pair:
             copy.start()
-    build_powers(unit, mix_ref, power_ref)
+    prepare()
+    for copy in lon_faces:
+        copy.wait()
+    prepare_outer()
     for pair in first[:2]:
         for copy in pair:
             copy.wait()
     lon_sweep(x_ref, mid_ref, 0, 2 * edge, edge_row)
     lat_start(mid_ref, 0)
+    prepare_rates()
+    build_powers(unit, mix_ref, power_ref)
+
+    @pl.when(has_south)
+    def _():
+        for copy in lat_faces:
+            copy.wait_send()
+
+    @pl.when(has_north)
+    def _():
+        for copy in lat_faces:
+            copy.wait_recv()
+
+    prepare_north()
     for copy in first[2]:
         copy.wait()
     lon_sweep(x_ref, mid_ref, 0, inner, inner_row)
@@ -332,16 +445,6 @@
     lat_sweep(again_ref, out_ref, 1, edge_spans)
 
 
-def shifted(value, axis, steps):
-    count = lax.axis_size(axis)
-    return lax.ppermute(value, axis, [(i, (i + steps) % count) for i in range(count)])
-
-
-def from_ahead(value, axis):
-    count = lax.axis_size(axis)
-    return lax.ppermute(value, axis, [(i + 1, i) for i in range(count - 1)])
-
-
 def slopes(c, m):
     return jnp.where(c >= 0.0, 0.5 * (1.0 - c), -0.5 * (1.0 + c)) * m
 
@@ -360,32 +463,8 @@
 ):
     species, rows, lanes = tracers.shape
     levels = level_light.shape[0]
-    columns = lanes // levels
     unit = 2 * levels
-    f32 = jnp.float32
-    nlat = lax.axis_size("lat")
-    faces = jnp.concatenate([courant, switches.astype(f32)], 0)
-    east_faces = shifted(faces[0::2, :, :1], "lon", -1)
-    north_faces = from_ahead(faces[1::2, :1], "lat")
-    lon_faces = jnp.concatenate([faces[0::2], east_faces, east_faces], 2)
-    lat_faces = jnp.concatenate([faces[1::2], north_faces], 1)
-    global_face = lax.axis_index("lat") * rows + jnp.arange(rows + 1, dtype=jnp.int32)
-    valid = ((global_face >= 1) & (global_face < rows * nlat)).astype(f32)[:, None]
-    lat_c = lat_faces[0] * valid
-    spread = functools.partial(jnp.repeat, repeats=levels, axis=-1)
-    lon_c = spread(lon_faces[0])
-    lon_k = spread(slopes(lon_faces[0], lon_faces[1]))
-    lat_k = spread(slopes(lat_c, lat_faces[1]))
-    lat_c = spread(lat_c)
-    sun = spread(day_flags.astype(f32)) * jnp.tile(level_light, columns)
-    counts = spread(diffusion_counts)
-    mixing = jnp.concatenate([vertical_mixing, jnp.zeros((1,), f32)])
-    mixing = jnp.tile(mixing, 2)[None]
-    rates = jnp.concatenate([night_rates, photo_rates], 0)
-    top = lax.reduce_precision(rates, 8, 7)
-    rest = (rates - top).astype(jnp.bfloat16)
-    top = top.astype(jnp.bfloat16)
-    weights = jnp.concatenate([top, top, rest], 1)
+    f32, i32, bf16 = jnp.float32, jnp.int32, jnp.bfloat16
     block = (rows, species, lanes)
     out = pl.pallas_call(
         functools.partial(kernel, unit),
@@ -393,6 +472,17 @@
         in_specs=[pl.BlockSpec(memory_space=pltpu.VMEM)] * 10,
         out_specs=pl.BlockSpec(memory_space=pltpu.VMEM),
         scratch_shapes=[
+            pltpu.VMEM((rows, 1, lanes + unit), f32),
+            pltpu.VMEM((rows, 1, lanes + unit), f32),
+            pltpu.VMEM((rows + 1, 1, lanes), f32),
+            pltpu.VMEM((rows + 1, 1, lanes), f32),
+            pltpu.VMEM((rows, 1, lanes), f32),
+            pltpu.VMEM((rows, 1, lanes), i32),
+            pltpu.VMEM((1, unit), f32),
+            pltpu.VMEM((2 * species, 3 * species), bf16),
+            pltpu.VMEM((species, 1), f32),
+            pltpu.VMEM((2,) + courant.shape, f32),
+            pltpu.VMEM((2,) + switches.shape, i32),
             pltpu.VMEM(block, f32),
             pltpu.VMEM(block, f32),
             pltpu.VMEM(block, f32),
@@ -400,9 +490,11 @@
             pltpu.VMEM((2, rows, species, unit), f32),
             pltpu.VMEM((2, 2, species, lanes), f32),
             pltpu.VMEM((2, 2, species, lanes), f32),
-            pltpu.VMEM((3 * unit, KMAX * unit), jnp.bfloat16),
+            pltpu.VMEM((3 * unit, KMAX * unit), bf16),
             pltpu.SemaphoreType.DMA((2, 3, 2)),
             pltpu.SemaphoreType.DMA((2, 3, 2)),
+            pltpu.SemaphoreType.DMA((2, 2)),
+            pltpu.SemaphoreType.DMA((2, 2)),
             pltpu.SemaphoreType.DMA((2, 2)),
             pltpu.SemaphoreType.DMA((2, 2)),
         ],
@@ -411,15 +503,15 @@
         ),
     )(
         jnp.transpose(tracers, (1, 0, 2)),
-        lon_c[:, None],
-        lon_k[:, None],
-        lat_c[:, None],
-        lat_k[:, None],
-        sun[:, None],
-        counts[:, None],
-        mixing,
-        weights,
-        self_loss[:, None],
+        courant,
+        switches,
+        day_flags,
+        diffusion_counts,
+        night_rates,
+        photo_rates,
+        level_light[None],
+        self_loss[None],
+        vertical_mixing[None],
     )
     return jnp.transpose(out, (1, 0, 2))
 

time: 88.1 us -> 75.2 us (0.85)
  starting transfers between devices: 5.85 us -> 0 us
  local copies, waits for them, and re-layouts: 10.4 us -> 5.47 us
  other arithmetic: 3.13 us -> 0 us
  Pallas kernels: 68 us -> 69.5 us
    ppermute x2 -> x0, starting transfers between devices: 5.85 us -> none  [the longest x1 4.57 us: shifted(): lax.ppermute(value, axis, [(i, (i + steps) % count) for i in range(count)])]
    broadcast_in_dim x7 -> x0, local copies, waits for them, and re-layouts: 1.98 us -> none  [the longest x1 0.78 us: shards(): counts = spread(diffusion_counts)]
    concatenate x4 -> x0, other arithmetic: 1.59 us -> none  [the longest x1 0.73 us: shards(): mixing = jnp.concatenate([vertical_mixing, jnp.zeros((1,), f32)])]
    pallas_call x1, Pallas kernels: 68 us -> 69.5 us  [shards(): pl.pallas_call(functools.partial(kernel, unit), out_shape=jax.ShapeDtypeS...]
    another operation x8 -> x0, local copies, waits for them, and re-layouts: 1.42 us -> none  [the longest x1 0.66 us: shards(): sun = spread(day_flags.astype(f32)) * jnp.tile(level_light, columns)]
    convert_element_type x4 -> x0, other arithmetic: 1.4 us -> none  [the longest x1 0.7 us: shards(): faces = jnp.concatenate([courant, switches.astype(f32)], 0)]
    unnamed x2 -> x19, local copies, waits for them, and re-layouts: 3.53 us -> 2.93 us
  transfers between devices with their start and end apart: 2 -> 0, of which waited for: 0 -> 0; matrix products, arithmetic and copies ran while one was open for 10% -> 0% of each run, Pallas kernels for 0% -> 0%
where the time goes in v2:
time: 75.2 us; the launch traced here: 75.1 us
  Pallas kernels  69.5 us (92%)
  local copies, waits for them, and re-layouts  5.47 us (7%)
    pallas_call x1, Pallas kernels, shards(): pl.pallas_call(functools.partial(kernel, unit), out_shape=jax.ShapeDtypeS...  69.5 us
    unnamed x19, local copies, waits for them, and re-layouts  2.93 us
    transpose x1, local copies, waits for them, and re-layouts, shards(): return jnp.transpose(out, (1, 0, 2))  2.54 us

profile of v2, /device:TPU:0, one launch (start us, length us, event | category | flops | bytes accessed | tf_op | source)
XLA Modules:
  0.0 75.1 jit_solution(6443706021006386987)
XLA Ops:
  0.0 0.0 copy-start
  0.0 0.0 copy-start.1
  0.0 0.0 copy-start.2
  0.0 0.0 copy-start.3
  0.0 0.0 copy-start.4
  0.0 0.0 copy-start.5
  0.0 0.0 copy-start.6
  0.0 0.0 copy-start.7
  0.0 0.0 copy-start.8
  0.1 2.9 %copy.14 = f32[32,8,2048]{2,0,1:T(8,128)S(1)} copy(f32[32,8,2048]{2,1,0:T(8,128)} %param.10) | data formatting | bytes 4194304 | tf_op args[0]
  3.0 0.0 copy-done
  3.0 0.0 copy-done.1
  3.0 0.0 copy-done.2
  3.0 0.0 copy-done.3
  3.0 0.0 copy-done.4
  3.0 0.0 copy-done.5
  3.0 0.0 copy-done.6
  3.0 0.0 copy-done.7
  3.0 0.0 copy-done.8
  3.0 69.5 %shard_map.100 = f32[8,32,2048]{2,1,0:T(8,128)S(1)} custom-call(f32[8,32,2048]{2,1,0:T(8,128)S(1)} %bitcast.8, f32[2,8,32]{2,1,0:T(8,128)S(1)} %copy-done.2, s32[2,8,32]{2,1,0:T(8,128)S(1)} %copy-done.3, s32[8,32]{1,0:T(8,128)S(1)} %copy-done.4, s32[8,32]{1,0:T(8,128)S(1)} %copy-done.5, f32[32,32]{1,0:T(8,128)S(1)} %copy-done, f32[32,32]{1,0:T(8,128)S(1)} %copy-done.1, ...), custom_call_target="tpu_custom_call" | custom-call | tf_op jit(solution)/shard_map/pallas_call | solution.py:469
  72.5 2.5 %copy.12 = f32[32,8,2048]{2,1,0:T(8,128)} copy(f32[32,8,2048]{2,0,1:T(8,128)S(1)} %bitcast.7) | data formatting | bytes 4194304 | tf_op jit(solution)/shard_map/transpose | solution.py:516
Async XLA Ops:
  0.0 3.0 %copy-start = (f32[32,32]{1,0:T(8,128)S(1)}, f32[32,32]{1,0:T(8,128)}, u32[]{:S(2)}) copy-start(f32[32,32]{1,0:T(8,128)} %night_ref.1) | copy-start | bytes 12292
  0.0 3.0 %copy-start.1 = (f32[32,32]{1,0:T(8,128)S(1)}, f32[32,32]{1,0:T(8,128)}, u32[]{:S(2)}) copy-start(f32[32,32]{1,0:T(8,128)} %photo_ref.1) | copy-start | bytes 12292
  0.0 3.0 %copy-start.2 = (f32[2,8,32]{2,1,0:T(8,128)S(1)}, f32[2,8,32]{2,1,0:T(8,128)}, u32[]{:S(2)}) copy-start(f32[2,8,32]{2,1,0:T(8,128)} %courant_ref.1) | copy-start | bytes 6148
  0.0 3.0 %copy-start.3 = (s32[2,8,32]{2,1,0:T(8,128)S(1)}, s32[2,8,32]{2,1,0:T(8,128)}, u32[]{:S(2)}) copy-start(s32[2,8,32]{2,1,0:T(8,128)} %switch_ref.1) | copy-start | bytes 6148
  0.0 3.0 %copy-start.4 = (s32[8,32]{1,0:T(8,128)S(1)}, s32[8,32]{1,0:T(8,128)}, u32[]{:S(2)}) copy-start(s32[8,32]{1,0:T(8,128)} %day_ref.1) | copy-start | bytes 3076
  0.0 3.0 %copy-start.5 = (s32[8,32]{1,0:T(8,128)S(1)}, s32[8,32]{1,0:T(8,128)}, u32[]{:S(2)}) copy-start(s32[8,32]{1,0:T(8,128)} %raw_cnt_ref.1) | copy-start | bytes 3076
  0.0 3.0 %copy-start.6 = (f32[64]{0:T(128)S(1)}, f32[64]{0:T(128)}, u32[]{:S(2)}) copy-start(f32[64]{0:T(128)} %param.17) | copy-start | bytes 772
  0.0 3.0 %copy-start.7 = (f32[32]{0:T(128)S(1)}, f32[32]{0:T(128)}, u32[]{:S(2)}) copy-start(f32[32]{0:T(128)} %param.18) | copy-start | bytes 388
  0.0 3.0 %copy-start.8 = (f32[63]{0:T(128)S(1)}, f32[63]{0:T(128)}, u32[]{:S(2)}) copy-start(f32[63]{0:T(128)} %param.19) | copy-start | bytes 760

commit v3 on v2

--- a/solution.py
+++ b/solution.py
@@ -94,6 +94,7 @@
     lon, lat = lax.axis_index("lon"), lax.axis_index("lat")
     east, west = lax.rem(lon + 1, nlon), lax.rem(lon + nlon - 1, nlon)
     has_south, has_north = lat > 0, lat < nlat - 1
+    lower_half = lat < nlat // 2
 
     barrier = pltpu.get_barrier_semaphore()
     for side in (east, west):
@@ -239,7 +240,7 @@
     def lat_start(source, turn):
         up, down = lat_copies(source, turn)
 
-        @pl.when(has_north)
+        @pl.when(jnp.logical_and(has_north, lower_half))
         def _():
             up.start()
 
@@ -247,18 +248,27 @@
         def _():
             down.start()
 
-    def lat_wait(source, turn):
+        @pl.when(jnp.logical_and(has_north, jnp.logical_not(lower_half)))
+        def _():
+            up.start()
+
+    def lat_arrive(source, turn, side):
+        up, down = lat_copies(source, turn)
+
+        @pl.when(has_north if side else has_south)
+        def _():
+            (down if side else up).wait_recv()
+
+    def lat_sent(source, turn):
         up, down = lat_copies(source, turn)
 
         @pl.when(has_north)
         def _():
             up.wait_send()
-            down.wait_recv()
 
         @pl.when(has_south)
         def _():
             down.wait_send()
-            up.wait_recv()
 
     def edge_row(i):
         return i + (i // edge) * (rows - 2 * edge)
@@ -426,12 +436,24 @@
     second = [lon_copies(state_ref, 1, group) for group in range(3)]
     for copy in second[2]:
         copy.start()
-    lat_wait(mid_ref, 0)
-    lat_sweep(mid_ref, state_ref, 0, edge_spans)
-    chemistry(2 * edge, edge_row)
-    for pair in second[:2]:
-        for copy in pair:
+
+    def finish_edge(side):
+        lat_arrive(mid_ref, 0, side)
+        lat_sweep(mid_ref, state_ref, 0, (edge_spans[side],))
+        chemistry(edge, lambda i: i + side * (rows - edge))
+        for copy in second[side]:
             copy.start()
+
+    @pl.when(lower_half)
+    def _():
+        finish_edge(0)
+        finish_edge(1)
+
+    @pl.when(jnp.logical_not(lower_half))
+    def _():
+        finish_edge(1)
+        finish_edge(0)
+
     for pair in second[:2]:
         for copy in pair:
             copy.wait()
@@ -441,8 +463,11 @@
         copy.wait()
     lon_sweep(state_ref, again_ref, 1, inner, inner_row)
     lat_sweep(again_ref, out_ref, 1, inner_spans)
-    lat_wait(again_ref, 1)
-    lat_sweep(again_ref, out_ref, 1, edge_spans)
+    for side in range(2):
+        lat_arrive(again_ref, 1, side)
+        lat_sweep(again_ref, out_ref, 1, (edge_spans[side],))
+    lat_sent(mid_ref, 0)
+    lat_sent(again_ref, 1)
 
 
 def slopes(c, m):

time: 75.2 us -> 62.8 us (0.84)
  Pallas kernels: 69.5 us -> 57 us
    pallas_call x1, Pallas kernels: 69.5 us -> 57 us  [shards(): pl.pallas_call(functools.partial(kernel, unit), out_shape=jax.ShapeDtypeS...]
where the time goes in v3:
time: 62.8 us; the launch traced here: 62.6 us
  Pallas kernels  57 us (91%)
  local copies, waits for them, and re-layouts  5.47 us (9%)
    pallas_call x1, Pallas kernels, shards(): pl.pallas_call(functools.partial(kernel, unit), out_shape=jax.ShapeDtypeS...  57 us
    unnamed x19, local copies, waits for them, and re-layouts  2.93 us
    transpose x1, local copies, waits for them, and re-layouts, shards(): return jnp.transpose(out, (1, 0, 2))  2.54 us

profile of v3, /device:TPU:0, one launch (start us, length us, event | category | flops | bytes accessed | tf_op | source)
XLA Modules:
  0.0 62.6 jit_solution(8734259317408412844)
XLA Ops:
  0.0 0.0 copy-start
  0.0 0.0 copy-start.1
  0.0 0.0 copy-start.2
  0.0 0.0 copy-start.3
  0.0 0.0 copy-start.4
  0.0 0.0 copy-start.5
  0.0 0.0 copy-start.6
  0.0 0.0 copy-start.7
  0.0 0.0 copy-start.8
  0.1 2.9 %copy.14 = f32[32,8,2048]{2,0,1:T(8,128)S(1)} copy(f32[32,8,2048]{2,1,0:T(8,128)} %param.10) | data formatting | bytes 4194304 | tf_op args[0]
  3.0 0.0 copy-done
  3.0 0.0 copy-done.1
  3.0 0.0 copy-done.2
  3.0 0.0 copy-done.3
  3.0 0.0 copy-done.4
  3.0 0.0 copy-done.5
  3.0 0.0 copy-done.6
  3.0 0.0 copy-done.7
  3.0 0.0 copy-done.8
  3.0 57.0 %shard_map.100 = f32[8,32,2048]{2,1,0:T(8,128)S(1)} custom-call(f32[8,32,2048]{2,1,0:T(8,128)S(1)} %bitcast.8, f32[2,8,32]{2,1,0:T(8,128)S(1)} %copy-done.2, s32[2,8,32]{2,1,0:T(8,128)S(1)} %copy-done.3, s32[8,32]{1,0:T(8,128)S(1)} %copy-done.4, s32[8,32]{1,0:T(8,128)S(1)} %copy-done.5, f32[32,32]{1,0:T(8,128)S(1)} %copy-done, f32[32,32]{1,0:T(8,128)S(1)} %copy-done.1, ...), custom_call_target="tpu_custom_call" | custom-call | tf_op jit(solution)/shard_map/pallas_call | solution.py:494
  60.1 2.5 %copy.12 = f32[32,8,2048]{2,1,0:T(8,128)} copy(f32[32,8,2048]{2,0,1:T(8,128)S(1)} %bitcast.7) | data formatting | bytes 4194304 | tf_op jit(solution)/shard_map/transpose | solution.py:541
Async XLA Ops:
  0.0 3.0 %copy-start = (f32[32,32]{1,0:T(8,128)S(1)}, f32[32,32]{1,0:T(8,128)}, u32[]{:S(2)}) copy-start(f32[32,32]{1,0:T(8,128)} %night_ref.1) | copy-start | bytes 12292
  0.0 3.0 %copy-start.1 = (f32[32,32]{1,0:T(8,128)S(1)}, f32[32,32]{1,0:T(8,128)}, u32[]{:S(2)}) copy-start(f32[32,32]{1,0:T(8,128)} %photo_ref.1) | copy-start | bytes 12292
  0.0 3.0 %copy-start.2 = (f32[2,8,32]{2,1,0:T(8,128)S(1)}, f32[2,8,32]{2,1,0:T(8,128)}, u32[]{:S(2)}) copy-start(f32[2,8,32]{2,1,0:T(8,128)} %courant_ref.1) | copy-start | bytes 6148
  0.0 3.0 %copy-start.3 = (s32[2,8,32]{2,1,0:T(8,128)S(1)}, s32[2,8,32]{2,1,0:T(8,128)}, u32[]{:S(2)}) copy-start(s32[2,8,32]{2,1,0:T(8,128)} %switch_ref.1) | copy-start | bytes 6148
  0.0 3.0 %copy-start.4 = (s32[8,32]{1,0:T(8,128)S(1)}, s32[8,32]{1,0:T(8,128)}, u32[]{:S(2)}) copy-start(s32[8,32]{1,0:T(8,128)} %day_ref.1) | copy-start | bytes 3076
  0.0 3.0 %copy-start.5 = (s32[8,32]{1,0:T(8,128)S(1)}, s32[8,32]{1,0:T(8,128)}, u32[]{:S(2)}) copy-start(s32[8,32]{1,0:T(8,128)} %raw_cnt_ref.1) | copy-start | bytes 3076
  0.0 3.0 %copy-start.6 = (f32[64]{0:T(128)S(1)}, f32[64]{0:T(128)}, u32[]{:S(2)}) copy-start(f32[64]{0:T(128)} %param.17) | copy-start | bytes 772
  0.0 3.0 %copy-start.7 = (f32[32]{0:T(128)S(1)}, f32[32]{0:T(128)}, u32[]{:S(2)}) copy-start(f32[32]{0:T(128)} %param.18) | copy-start | bytes 388
  0.0 3.0 %copy-start.8 = (f32[63]{0:T(128)S(1)}, f32[63]{0:T(128)}, u32[]{:S(2)}) copy-start(f32[63]{0:T(128)} %param.19) | copy-start | bytes 760
